TPU v7x, 256 devices: a whole 4x4x8 slice. The times are simulated.
256 devices in a mesh: task: 8 (over z_hi, core), row: 8 (over x, z_lo), col: 4 (over y).
Axes of the slice: x: 4, y: 4, z: 8 (z_hi: 4, z_lo: 2; z = z_hi * 2 + z_lo), core: 2. Of those that a mesh axis runs over, the one named last changes fastest.
Arguments:
- activations: bfloat16 [8, 512, 13824], P('task', 'col', 'row'), may hold values from -6 to 6
- weights: bfloat16 [8, 13824, 5120], P('task', 'row', 'col'), may hold values from -0.0625 to 0.0625
- labels: int32 [8, 512], P('task'), may hold values from 0 to 127
- prototypes: bfloat16 [8, 128, 5120], P('task', None, 'col'), may hold values from -6 to 6
Outputs:
- merged: bfloat16 [13824, 5120], P('row', 'col')
- merged_out: bfloat16 [8, 512, 5120], P('task', 'row', 'col')
All inputs are finite; a program needn't handle non-finite values.
Results may differ from a plain program's by a relative error of at most 0.02.
Values may be sent and summed in bfloat16 or wider, within the bound.
A program may use at most 128 MiB of HBM per device.

v0:
```python
import jax
import jax.numpy as jnp
from jax import lax
from jax.sharding import PartitionSpec as P


def class_targets(label_rows, protos):
    count = label_rows.shape[0]
    onehot = (
        label_rows[:, None] == lax.broadcasted_iota(jnp.int32, (count, protos.shape[0]), 1)
    ).astype(jnp.bfloat16)
    return jnp.dot(onehot, protos, preferred_element_type=jnp.float32)


def local(activations, weights, labels, prototypes):
    acts = activations[0]
    weight = weights[0]
    label_row = labels[0]
    protos = prototypes[0]
    full_acts = lax.all_gather(acts, "col", axis=0, tiled=True)
    partial_out = jnp.dot(full_acts, weight, preferred_element_type=jnp.float32)
    output = lax.psum(partial_out.astype(jnp.bfloat16), "row").astype(jnp.float32)
    grad = output - class_targets(label_row, protos)
    gsq = (grad * grad).astype(jnp.bfloat16)
    wide = full_acts.astype(jnp.float32)
    asq = (wide * wide).astype(jnp.bfloat16)
    fisher = lax.dot_general(asq, gsq, (((0,), (0,)), ((), ())), preferred_element_type=jnp.float32)
    weighted = fisher * weight.astype(jnp.float32)
    numer, denom = (
        lax.psum_scatter(weighted, "task", scatter_dimension=0, tiled=True),
        lax.psum_scatter(fisher, "task", scatter_dimension=0, tiled=True),
    )
    piece = (numer / (denom + 1e-06)).astype(jnp.bfloat16)
    merged = lax.all_gather(piece, "task", axis=0, tiled=True)
    result = lax.psum_scatter(
        jnp.dot(full_acts, merged, preferred_element_type=jnp.float32).astype(jnp.bfloat16),
        "row",
        scatter_dimension=0,
        tiled=True,
    )
    return (merged, result[None])


def solution(mesh):
    placed = (
        P("task", "col", "row"),
        P("task", "row", "col"),
        P("task", None),
        P("task", None, "col"),
    )
    return jax.shard_map(
        local,
        mesh=mesh,
        in_specs=placed,
        out_specs=(P("row", "col"), P("task", "row", "col")),
        check_vma=False,
    )
```

profile of v0, /device:TPU:8, one launch (start us, length us, event | category | flops | bytes accessed | tf_op | source)
XLA Modules:
  0.0 475.8 jit_solution(1805810077636972893)
XLA Ops:
  7.2 0.0 all-gather.6.cloned.1.call-start
  7.2 0.7 all-gather.6.cloned.1.call-update
  7.9 0.0 all-reduce.2.cloned.1.call-start
  8.0 38.4 %all-gather.6.cloned.1.call-done = bf16[1,512,1728]{1,2,0:T(8,128)(2,1)} async-done(((bf16[1,128,1728]{1,2,0:T(8,128)(2,1)}), bf16[1,512,1728]{1,2,0:T(8,128)(2,1)}) %all-gather.6.cloned.1.call-update) | async-done | bytes 1769488 | tf_op jit(solution)/shard_map/all_gather | solution.py:20
  46.4 6.6 %fusion.4 = bf16[512,1280]{1,0:T(8,128)(2,1)} fusion(bf16[1,1728,1280]{2,1,0:T(8,128)(2,1)} %param.5, bf16[1,512,1728]{1,2,0:T(8,128)(2,1)} %all-gather.6.cloned.1.call-done), kind=kOutput, calls=%fused_computation.7 | convolution fusion | flops 2265579520 | bytes 7503872 | tf_op jit(solution)/shard_map/dot_general | solution.py:21
  53.0 0.0 all-reduce.2.cloned.1.call-update
  53.0 0.0 reduce-scatter.6.cloned.1.call-start
  53.1 90.5 %all-reduce.2.cloned.1.call-done = bf16[512,1280]{1,0:T(8,128)(2,1)} async-done(((bf16[512,1280]{1,0:T(8,128)(2,1)}), bf16[512,1280]{1,0:T(8,128)(2,1)}) %all-reduce.2.cloned.1.call-update) | async-done | bytes 1310736 | tf_op jit(solution)/shard_map/psum | solution.py:22
  143.6 9.8 %convert_multiply_fusion = (f32[1728,1280]{1,0:T(8,128)}, f32[1728,1280]{1,0:T(8,128)}) fusion(bf16[1,1728,1280]{2,1,0:T(8,128)(2,1)} %param.5, bf16[512,1280]{1,0:T(8,128)(2,1)} %all-reduce.2.cloned.1.call-done, bf16[1,128,1280]{2,1,0:T(8,128)(2,1)S(1)} %copy-done, s32[512]{0:T(512)S(1)} %bitcast.30, bf16[1,512,1728]{1,2,0:T(8,128)(2,1)S(1)} %copy-done.1), kind=kOutput, calls=%fused_computation | convolution fusion | flops 2442461184 | bytes 25528320 | tf_op jit(solution)/shard_map/dot_general | solution.py:27
  153.4 0.0 reduce-scatter.6.cloned.1.call-update
  153.4 0.0 reduce-scatter.8.cloned.1.call-start
  153.4 0.5 reduce-scatter.8.cloned.1.call-update
  154.0 0.0 all-gather.4.cloned.1.call-start
  154.0 96.8 %reduce-scatter.6.cloned.1.call-done = f32[216,1280]{1,0:T(8,128)} async-done(((f32[1728,1280]{1,0:T(8,128)}), f32[216,1280]{1,0:T(8,128)}) %reduce-scatter.6.cloned.1.call-update) | async-done | bytes 1105936 | tf_op jit(solution)/shard_map/reduce_scatter | solution.py:30
  250.8 104.8 %reduce-scatter.8.cloned.1.call-done = f32[216,1280]{1,0:T(8,128)} async-done(((f32[1728,1280]{1,0:T(8,128)}), f32[216,1280]{1,0:T(8,128)}) %reduce-scatter.8.cloned.1.call-update) | async-done | bytes 1105936 | tf_op jit(solution)/shard_map/reduce_scatter | solution.py:31
  355.7 2.5 divide_convert_fusion
  358.2 0.0 reduce-scatter.10.cloned.1.call-start
  358.3 54.9 %all-gather.4.cloned.1.call-done = bf16[1728,1280]{1,0:T(8,128)(2,1)} async-done(((bf16[216,1280]{1,0:T(8,128)(2,1)}), bf16[1728,1280]{1,0:T(8,128)(2,1)}) %all-gather.4.cloned.1.call-update) | async-done | bytes 4423696 | tf_op jit(solution)/shard_map/all_gather | solution.py:34
  413.1 4.8 %fusion.7 = bf16[512,1280]{0,1:T(8,128)(2,1)S(1)} fusion(bf16[1728,1280]{1,0:T(8,128)(2,1)} %all-gather.4.cloned.1.call-done, bf16[1,512,1728]{1,2,0:T(8,128)(2,1)S(1)} %copy-done.1), kind=kOutput, calls=%fused_computation.9 | convolution fusion | flops 2265579520 | bytes 7503872 | tf_op jit(solution)/shard_map/dot_general | solution.py:36
  418.0 1.4 copy.8
  419.4 42.9 %reduce-scatter.10.cloned.1.call-done = bf16[64,1280]{1,0:T(8,128)(2,1)} async-done(((bf16[512,1280]{1,0:T(8,128)(2,1)}), bf16[64,1280]{1,0:T(8,128)(2,1)}) %reduce-scatter.10.cloned.1.call-update) | async-done | bytes 163856
  462.4 1.1 copy.9
  463.5 0.8 copy.7
  464.3 4.6 copy.12
  (8 shorter events, 0.0 us)
Async XLA Ops:
  7.2 136.4 %copy-start = (bf16[1,128,1280]{2,1,0:T(8,128)(2,1)S(1)}, bf16[1,128,1280]{2,1,0:T(8,128)(2,1)}, u32[]{:S(2)}) copy-start(bf16[1,128,1280]{2,1,0:T(8,128)(2,1)} %param.7) | copy-start | bytes 983044
  7.2 39.2 %all-gather.6.cloned.1.call-start = ((), (), s32[]{:S(2)}) async-start(), calls=%async_computation.7 | async-start | bytes 2211840 | tf_op jit(solution)/shard_map/all_gather | solution.py:20
  7.9 135.7 %copy-start.2 = (s32[1,512]{1,0:T(1,128)S(1)}, s32[1,512]{1,0:T(1,128)}, u32[]{:S(2)}) copy-start(s32[1,512]{1,0:T(1,128)} %param.6) | copy-start | bytes 6148
  7.9 135.7 %all-reduce.2.cloned.1.call-start = ((), (), s32[]{:S(2)}) async-start(), calls=%async_computation.3 | async-start | bytes 2621440 | tf_op jit(solution)/shard_map/psum | solution.py:22
  46.4 97.2 %copy-start.1 = (bf16[1,512,1728]{1,2,0:T(8,128)(2,1)S(1)}, bf16[1,512,1728]{1,2,0:T(8,128)(2,1)}, u32[]{:S(2)}) copy-start(bf16[1,512,1728]{1,2,0:T(8,128)(2,1)} %all-gather.6.cloned.1.call-done) | copy-start | bytes 5308420
  53.0 197.8 %reduce-scatter.6.cloned.1.call-start = ((), (), s32[]{:S(2)}) async-start(), calls=%async_computation.4 | async-start | bytes 9953280 | tf_op jit(solution)/shard_map/reduce_scatter | solution.py:30
  153.4 202.3 %reduce-scatter.8.cloned.1.call-start = ((), (), s32[]{:S(2)}) async-start(), calls=%async_computation.5 | async-start | bytes 9953280 | tf_op jit(solution)/shard_map/reduce_scatter | solution.py:31
  154.0 259.2 %all-gather.4.cloned.1.call-start = ((), (), s32[]{:S(2)}) async-start(), calls=%async_computation.6 | async-start | bytes 4976640 | tf_op jit(solution)/shard_map/all_gather | solution.py:34
  358.2 104.1 %reduce-scatter.10.cloned.1.call-start = ((), (), s32[]{:S(2)}) async-start(), calls=%async_computation.8 | async-start | bytes 1474560
Sparse Core Ops, SparseCore 0:
  9.8 36.5 all-gather.5
  53.1 90.4 all-reduce.1
  153.5 97.2 reduce-scatter.5
  253.4 102.1 reduce-scatter.7
  358.3 54.7 all-gather.3
  419.6 42.7 reduce-scatter.9
where the time goes:
time: 476 us
  waiting for transfers between devices  430 us (90%)
  matrix products  21.2 us (4%)
  between operations  14.1 us (3%)
  local copies, waits for them, and re-layouts  8.06 us (2%)
    reduce_scatter x1, waiting for transfers between devices, local(): lax.psum_scatter(fisher, 'task', scatter_dimension=0, tiled=True)  105 us
    reduce_scatter x1, waiting for transfers between devices, local(): lax.psum_scatter(weighted, 'task', scatter_dimension=0, tiled=True)  96.8 us
    psum x1, waiting for transfers between devices, local(): lax.psum(partial_out.astype(jnp.bfloat16), 'row').astype(jnp.float32)  90.5 us
    all_gather x1, waiting for transfers between devices, local(): merged = lax.all_gather(piece, 'task', axis=0, tiled=True)  54.9 us
    unnamed x7, waiting for transfers between devices  44.2 us
    all_gather x1, waiting for transfers between devices, local(): full_acts = lax.all_gather(acts, 'col', axis=0, tiled=True)  38.4 us
    dot_general x1, matrix products, local(): lax.dot_general(asq, gsq, (((0,), (0,)), ((), ())), preferred_element_typ...  9.77 us
  transfers between devices with their start and end apart: 6, of which 6 were waited for; matrix products, arithmetic and copies ran while one was open for 0% of the time, Pallas kernels for 0%

commit v1 on v0

--- a/solution.py
+++ b/solution.py
@@ -17,7 +17,22 @@
     weight = weights[0]
     label_row = labels[0]
     protos = prototypes[0]
-    full_acts = lax.all_gather(acts, "col", axis=0, tiled=True)
+    ways, here, step = (lax.axis_size("col"), lax.axis_index("col"), acts.shape[0])
+    dims = [n * ways if d == 0 else n for d, n in enumerate(acts.shape)]
+    full_acts = lax.dynamic_update_slice_in_dim(
+        jnp.zeros(dims, acts.dtype), acts, here * step, axis=0
+    )
+    going_up = going_down = acts
+    for far in range(1, ways // 2 + 1):
+        going_up = lax.ppermute(going_up, "col", [(d, (d + 1) % ways) for d in range(ways)])
+        full_acts = lax.dynamic_update_slice_in_dim(
+            full_acts, going_up, (here - far) % ways * step, axis=0
+        )
+        if 2 * far < ways:
+            going_down = lax.ppermute(going_down, "col", [(d, (d - 1) % ways) for d in range(ways)])
+            full_acts = lax.dynamic_update_slice_in_dim(
+                full_acts, going_down, (here + far) % ways * step, axis=0
+            )
     partial_out = jnp.dot(full_acts, weight, preferred_element_type=jnp.float32)
     output = lax.psum(partial_out.astype(jnp.bfloat16), "row").astype(jnp.float32)
     grad = output - class_targets(label_row, protos)

time: 476 us -> 458 us (0.962)
  waiting for transfers between devices: 430 us -> 411 us
    unnamed x7 -> x5, waiting for transfers between devices: 44.2 us -> 0.75 us
    reduce_scatter x0 -> x1, waiting for transfers between devices: none -> 42.9 us  [local(): lax.psum_scatter(jnp.dot(full_acts, merged, preferred_element_type=jnp.fl...]
    all_gather x1 -> x0, waiting for transfers between devices: 38.4 us -> none  [local(): full_acts = lax.all_gather(acts, 'col', axis=0, tiled=True)]
    ppermute x0 -> x3, waiting for transfers between devices: none -> 18.6 us  [the longest x2 18.6 us: local(): lax.ppermute(going_up, 'col', [(d, (d + 1) % ways) for d in range(ways)])]
  transfers between devices with their start and end apart: 6 -> 8, of which waited for: 6 -> 7; matrix products, arithmetic and copies ran while one was open for 0% -> 0% of each run, Pallas kernels for 0% -> 0%
where the time goes in v1:
time: 458 us
  waiting for transfers between devices  411 us (90%)
  matrix products  21.6 us (5%)
  between operations  13.9 us (3%)
  local copies, waits for them, and re-layouts  5.2 us (1%)
    reduce_scatter x1, waiting for transfers between devices, local(): lax.psum_scatter(fisher, 'task', scatter_dimension=0, tiled=True)  104 us
    reduce_scatter x1, waiting for transfers between devices, local(): lax.psum_scatter(weighted, 'task', scatter_dimension=0, tiled=True)  96 us
    psum x1, waiting for transfers between devices, local(): lax.psum(partial_out.astype(jnp.bfloat16), 'row').astype(jnp.float32)  91.8 us
    all_gather x1, waiting for transfers between devices, local(): merged = lax.all_gather(piece, 'task', axis=0, tiled=True)  56.4 us
    reduce_scatter x1, waiting for transfers between devices, local(): lax.psum_scatter(jnp.dot(full_acts, merged, preferred_element_type=jnp.fl...  42.9 us
    ppermute x2, waiting for transfers between devices, local(): lax.ppermute(going_up, 'col', [(d, (d + 1) % ways) for d in range(ways)])  18.6 us
    dot_general x1, matrix products, local(): lax.dot_general(asq, gsq, (((0,), (0,)), ((), ())), preferred_element_typ...  9.77 us
  transfers between devices with their start and end apart: 8, of which 7 were waited for; matrix products, arithmetic and copies ran while one was open for 0% of the time, Pallas kernels for 0%

profile of v1, /device:TPU:8, one launch (start us, length us, event | category | flops | bytes accessed | tf_op | source)
XLA Modules:
  0.0 458.2 jit_solution(16461146961834436043)
XLA Ops:
  7.2 1.7 collective-permute-start
  8.9 0.7 collective-permute-start.1
  9.6 0.1 broadcast_in_dim.6
  9.7 0.1 constant_dynamic-update-slice_fusion.3
  9.9 9.5 %collective-permute-done = bf16[128,1728]{0,1:T(8,128)(2,1)S(1)} collective-permute-done((bf16[128,1728]{0,1:T(8,128)(2,1)}, bf16[128,1728]{0,1:T(8,128)(2,1)S(1)}, u32[]{:S(2)}, u32[]{:S(2)}) %collective-permute-start) | collective-permute-done | bytes 442400 | tf_op jit(solution)/shard_map/ppermute | solution.py:27
  19.4 1.6 collective-permute-start.2
  21.0 0.1 constant_dynamic-update-slice_fusion.2
  21.1 0.1 constant_dynamic-update-slice_fusion.1
  21.2 9.0 %collective-permute-done.2 = bf16[128,1728]{0,1:T(8,128)(2,1)S(1)} collective-permute-done((bf16[128,1728]{0,1:T(8,128)(2,1)S(1)}, bf16[128,1728]{0,1:T(8,128)(2,1)S(1)}, u32[]{:S(2)}, u32[]{:S(2)}) %collective-permute-start.2) | collective-permute-done | bytes 442400 | tf_op jit(solution)/shard_map/ppermute | solution.py:27
  30.3 0.1 constant_dynamic-update-slice_fusion
  30.4 5.9 %fusion.2 = bf16[512,1280]{1,0:T(8,128)(2,1)} fusion(bf16[512,1728]{0,1:T(8,128)(2,1)S(1)} %constant_dynamic-update-slice_fusion, bf16[1,1728,1280]{2,1,0:T(8,128)(2,1)} %param.5), kind=kOutput, calls=%fused_computation.4 | convolution fusion | flops 2265579520 | bytes 7503872 | tf_op jit(solution)/shard_map/dot_general | solution.py:36
  36.3 0.0 reduce-scatter.4.cloned.1.call-start
  36.4 91.8 %all-reduce.2.cloned.1.call-done = bf16[512,1280]{1,0:T(8,128)(2,1)} async-done(((bf16[512,1280]{1,0:T(8,128)(2,1)}), bf16[512,1280]{1,0:T(8,128)(2,1)}) %all-reduce.2.cloned.1.call-update) | async-done | bytes 1310736 | tf_op jit(solution)/shard_map/psum | solution.py:37
  128.2 9.8 %convert_multiply_fusion = (f32[1728,1280]{1,0:T(8,128)}, f32[1728,1280]{1,0:T(8,128)}) fusion(bf16[1,1728,1280]{2,1,0:T(8,128)(2,1)} %param.5, bf16[512,1280]{1,0:T(8,128)(2,1)} %all-reduce.2.cloned.1.call-done, bf16[1,128,1280]{2,1,0:T(8,128)(2,1)S(1)} %copy-done, s32[512]{0:T(512)S(1)} %bitcast.21, bf16[512,1728]{0,1:T(8,128)(2,1)S(1)} %constant_dynamic-update-slice_fusion), kind=kOutput, calls=%fused_computation | convolution fusion | flops 2442461184 | bytes 25528320 | tf_op jit(solution)/shard_map/dot_general | solution.py:42
  138.0 0.0 reduce-scatter.6.cloned.1.call-start
  138.0 0.7 reduce-scatter.6.cloned.1.call-update
  138.8 96.0 %reduce-scatter.4.cloned.1.call-done = f32[216,1280]{1,0:T(8,128)} async-done(((f32[1728,1280]{1,0:T(8,128)}), f32[216,1280]{1,0:T(8,128)}) %reduce-scatter.4.cloned.1.call-update) | async-done | bytes 1105936 | tf_op jit(solution)/shard_map/reduce_scatter | solution.py:45
  234.8 104.4 %reduce-scatter.6.cloned.1.call-done = f32[216,1280]{1,0:T(8,128)} async-done(((f32[1728,1280]{1,0:T(8,128)}), f32[216,1280]{1,0:T(8,128)}) %reduce-scatter.6.cloned.1.call-update) | async-done | bytes 1105936 | tf_op jit(solution)/shard_map/reduce_scatter | solution.py:46
  339.2 2.5 divide_convert_fusion
  341.8 0.0 reduce-scatter.8.cloned.1.call-start
  341.8 56.4 %all-gather.2.cloned.1.call-done = bf16[1728,1280]{1,0:T(8,128)(2,1)} async-done(((bf16[216,1280]{1,0:T(8,128)(2,1)}), bf16[1728,1280]{1,0:T(8,128)(2,1)}) %all-gather.2.cloned.1.call-update) | async-done | bytes 4423696 | tf_op jit(solution)/shard_map/all_gather | solution.py:49
  398.2 5.9 %convolution_convert_fusion = bf16[512,1280]{1,0:T(8,128)(2,1)} fusion(bf16[512,1728]{0,1:T(8,128)(2,1)S(1)} %constant_dynamic-update-slice_fusion, bf16[1728,1280]{1,0:T(8,128)(2,1)} %all-gather.2.cloned.1.call-done), kind=kOutput, calls=%fused_computation.5 | convolution fusion | flops 2265579520 | bytes 7503872 | tf_op jit(solution)/shard_map/dot_general | solution.py:51
  404.1 42.9 %reduce-scatter.8.cloned.1.call-done = bf16[64,1280]{1,0:T(8,128)(2,1)} async-done(((bf16[512,1280]{1,0:T(8,128)(2,1)}), bf16[64,1280]{1,0:T(8,128)(2,1)}) %reduce-scatter.8.cloned.1.call-update) | async-done | bytes 163856 | tf_op jit(solution)/shard_map/reduce_scatter | solution.py:50
  447.0 4.6 %copy.12 = bf16[1728,1280]{1,0:T(8,128)(2,1)} copy(bf16[1728,1280]{1,0:T(8,128)(2,1)} %all-gather.2.cloned.1.call-done) | data formatting | bytes 8847360
  (13 shorter events, 0.2 us)
Async XLA Ops:
  7.2 121.0 %copy-start = (bf16[1,128,1280]{2,1,0:T(8,128)(2,1)S(1)}, bf16[1,128,1280]{2,1,0:T(8,128)(2,1)}, u32[]{:S(2)}) copy-start(bf16[1,128,1280]{2,1,0:T(8,128)(2,1)} %param.7) | copy-start | bytes 983044
  7.2 2.5 copy-start.1
  7.2 121.0 %all-reduce.2.cloned.1.call-start = ((), (), s32[]{:S(2)}) async-start(), calls=%async_computation.3 | async-start | bytes 2621440 | tf_op jit(solution)/shard_map/psum | solution.py:37
  7.2 12.2 %collective-permute-start = (bf16[128,1728]{0,1:T(8,128)(2,1)}, bf16[128,1728]{0,1:T(8,128)(2,1)S(1)}, u32[]{:S(2)}, u32[]{:S(2)}) collective-permute-start(bf16[128,1728]{0,1:T(8,128)(2,1)} %bitcast.19), channel_id=1, source_target_pairs={{0,1},{1,2},{2,3},{3,0},{4,5},{5,6},{6,7},{7,4},{8,9},{9,10},{10,1... | collective-permute-start | bytes 1327112 | tf_op jit(solution)/shard_map/ppermute | solution.py:27
  8.9 12.2 %collective-permute-start.1 = (bf16[128,1728]{0,1:T(8,128)(2,1)}, bf16[128,1728]{0,1:T(8,128)(2,1)S(1)}, u32[]{:S(2)}, u32[]{:S(2)}) collective-permute-start(bf16[128,1728]{0,1:T(8,128)(2,1)} %bitcast.20), channel_id=1, source_target_pairs={{0,3},{1,0},{2,1},{3,2},{4,7},{5,4},{6,5},{7,6},{8,11},{9,8},{10,9... | collective-permute-start | bytes 1327112 | tf_op jit(solution)/shard_map/ppermute | solution.py:32
  19.4 10.8 %collective-permute-start.2 = (bf16[128,1728]{0,1:T(8,128)(2,1)S(1)}, bf16[128,1728]{0,1:T(8,128)(2,1)S(1)}, u32[]{:S(2)}, u32[]{:S(2)}) collective-permute-start(bf16[128,1728]{0,1:T(8,128)(2,1)S(1)} %collective-permute-done), channel_id=1, source_target_pairs={{0,1},{1,2},{2,3},{3,0},{4,5},{5,6},{6,7},{7,4},{8,9},{9,10},{10,1... | collective-permute-start | bytes 1327112 | tf_op jit(solution)/shard_map/ppermute | solution.py:27
  30.4 97.8 %copy-start.2 = (s32[1,512]{1,0:T(1,128)S(1)}, s32[1,512]{1,0:T(1,128)}, u32[]{:S(2)}) copy-start(s32[1,512]{1,0:T(1,128)} %param.6) | copy-start | bytes 6148
  36.3 198.4 %reduce-scatter.4.cloned.1.call-start = ((), (), s32[]{:S(2)}) async-start(), calls=%async_computation.4 | async-start | bytes 9953280 | tf_op jit(solution)/shard_map/reduce_scatter | solution.py:45
  138.0 201.2 %reduce-scatter.6.cloned.1.call-start = ((), (), s32[]{:S(2)}) async-start(), calls=%async_computation.5 | async-start | bytes 9953280 | tf_op jit(solution)/shard_map/reduce_scatter | solution.py:46
  138.7 259.4 %all-gather.2.cloned.1.call-start = ((), (), s32[]{:S(2)}) async-start(), calls=%async_computation.6 | async-start | bytes 4976640 | tf_op jit(solution)/shard_map/all_gather | solution.py:49
  341.8 105.3 %reduce-scatter.8.cloned.1.call-start = ((), (), s32[]{:S(2)}) async-start(), calls=%async_computation.7 | async-start | bytes 1474560 | tf_op jit(solution)/shard_map/reduce_scatter | solution.py:50
Sparse Core Ops, SparseCore 0:
  36.5 91.6 all-reduce.1
  138.1 96.6 reduce-scatter.3
  237.5 101.6 reduce-scatter.5
  341.9 56.2 all-gather.1
  404.2 42.7 reduce-scatter.7
